TPU v7x, 512 devices: a whole 4x4x16 slice. The times are simulated.
512 devices in a mesh: dp: 8 (over y, core), rot: 64 (over z, x).
Axes of the slice: x: 4, y: 4, z: 16, core: 2. Of those that a mesh axis runs over, the one named last changes fastest.
Arguments:
- frames: int32 [128, 128, 512], P('dp'), may hold values from 0 to 8, as said below
- slices: float32 [128, 128, 512], P('rot'), may hold values from 0.125 to 8, as said below
Outputs:
- log_resp: float32 [128, 128, 512], P('dp', 'rot')
- new_slices: float32 [128, 128, 512], P('rot', 'dp')
Inputs may be any that keep to these rules, and one draw needn't show every extreme that they name: `frames`: photon counts; each frame has its own brightness level. `slices`: positive intensities.
All inputs are finite; a program needn't handle non-finite values.
Results may differ from a plain program's by a relative error of at most 0.0012.
Values sent between devices are 32-bit elements; how exact they have to be, the bound alone decides.
A program may use at most 64 MiB of HBM per device.

v0:
```python
import functools
import math

import jax
import jax.numpy as jnp
import numpy as np
from jax import lax
from jax.experimental import pallas as pl
from jax.experimental.pallas import tpu as pltpu
from jax.sharding import PartitionSpec as P

F32, BF16 = jnp.float32, jnp.bfloat16
MESH = pl.DeviceIdType.MESH
LANES = 128


def packed_tables(angles):
    half, quarter = angles // 2, angles // 4
    p, g = np.arange(half)[:, None], np.arange(quarter)[None, :]
    even_phase = 2.0 * np.pi * ((p * g) % half) / half
    even = np.concatenate([np.cos(even_phase), -np.sin(even_phase)], axis=1)
    even[:, quarter] = 1.0 - 2.0 * (np.arange(half) % 2)
    odd_phase = 2.0 * np.pi * ((p * (2 * g + 1)) % angles) / angles
    odd = np.concatenate([np.cos(odd_phase), -np.sin(odd_phase)], axis=1)
    parts = []
    for table in (even, odd):
        high = table.astype(BF16)
        parts += [high, (table - high.astype(np.float64)).astype(BF16)]
    forward = np.stack(parts)
    return forward, np.ascontiguousarray(forward.transpose(0, 2, 1))


def mm(a, b):
    return jnp.dot(a, b, preferred_element_type=F32)


def split(x):
    high = x.astype(BF16)
    return high, (x - high.astype(F32)).astype(BF16)


def mm3(x, high, low):
    xh, xl = split(x)
    return mm(xh, high) + mm(xl, high) + mm(xh, low)


def lse_of(rows):
    top = functools.reduce(jnp.maximum, rows)
    return top + jnp.log(functools.reduce(jnp.add, [jnp.exp(r - top) for r in rows]))


def kernel(
    nx, frames, slices, ftab_hbm, itab_hbm, logp, new,
    fr, sl, ft, it, X, Y, acc, pb, sc, lsx, lsz, sa, ra, sb, rb,
    fsem, msem, xs, xr, zs, zr, as_, ar, bs, br,
):
    K, R, N = fr.shape
    T, H = sl.shape[0], N // 2
    dp, rot = lax.axis_index("dp"), lax.axis_index("rot")
    ny, nz = lax.axis_size("dp") // 2, lax.axis_size("rot") // nx
    y, core = dp // 2, dp % 2
    z, x = rot // nx, rot % nx
    share = R // (2 * ny)
    chunks = share // 8
    body = T * 4 * chunks

    c_ft = pltpu.make_async_copy(ftab_hbm, ft, msem.at[0])
    c_sl = pltpu.make_async_copy(slices, sl, msem.at[1])
    c_it = pltpu.make_async_copy(itab_hbm, it, msem.at[2])
    c_sl.start()
    c_ft.start()
    for k in range(K):
        pltpu.make_async_copy(frames.at[k], fr.at[k], fsem.at[k]).start()
    c_it.start()

    barrier = pltpu.get_barrier_semaphore()
    peers = [(dp, z * nx + (x + d) % nx) for d in range(1, nx)]
    peers += [(dp, ((z + d) % nz) * nx + x) for d in range(1, nz)]
    peers += [(y * 2 + 1 - core, rot)]
    peers += [(((y + d) % ny) * 2 + core, rot) for d in range(1, ny)]
    for peer in peers:
        pl.semaphore_signal(barrier, inc=1, device_id=peer, device_id_type=MESH)

    c_sl.wait()
    c_ft.wait()
    lane = lax.broadcasted_iota(jnp.int32, (R, LANES), 1)
    totals = []
    for t in range(T):
        values = sl[t]
        totals.append(jnp.sum(jnp.sum(values, axis=0, keepdims=True), axis=1, keepdims=True))
        logs = jnp.log(values)
        even, odd = logs[:, :H] + logs[:, H:], logs[:, :H] - logs[:, H:]
        eh, em = split(even)
        el = (even - eh.astype(F32) - em.astype(F32)).astype(BF16)
        ye = mm(eh, ft[0]) + mm(em, ft[0]) + mm(el, ft[0]) + mm(eh, ft[1])
        yo = mm3(odd, ft[2], ft[3])
        re, im = ye[:, :LANES], ye[:, LANES:]
        Y[t, 0] = re
        Y[t, 1] = jnp.where(lane == 0, 0.0, im)
        Y[t, 2] = jnp.where(lane == 0, im, re)
        Y[t, 3] = yo[:, :LANES]
        Y[t, 4] = yo[:, LANES:]

    @pl.loop(0, K)
    def _(k):
        pltpu.make_async_copy(frames.at[k], fr.at[k], fsem.at[k]).wait()
        left, right = fr[k, :, :H], fr[k, :, H:]
        xe = mm((left + right).astype(F32).astype(BF16), ft[0])
        xo = mm((left - right).astype(F32).astype(BF16), ft[2])
        X[k, 0] = xe[:, :LANES]
        X[k, 1] = xe[:, LANES:]
        X[k, 2] = xo[:, :LANES]
        X[k, 3] = xo[:, LANES:]
        sums = [None] * (4 * T)
        for c in range(R // 8):
            rows = slice(8 * c, 8 * c + 8)
            er, ei, o_r, oi = (X[k, j, rows] for j in range(4))
            for t in range(T):
                yr, yb, yc, zr_, zi = (Y[t, j, rows] for j in range(5))
                terms = (er * yr + ei * yb, ei * yc - er * yb, o_r * zr_ + oi * zi, oi * zr_ - o_r * zi)
                for j in range(4):
                    n = 4 * t + j
                    sums[n] = terms[j] if c == 0 else sums[n] + terms[j]
        for t in range(T):
            for j in range(4):
                acc[j, pl.ds(pl.multiple_of((t * K + k) * 8, 8), 8)] = sums[4 * t + j]

    rows = T * K
    lane = lax.broadcasted_iota(jnp.int32, (rows, LANES), 1)

    def gathered(j):
        return functools.reduce(
            jnp.add, [acc[j, pl.ds(s, rows, stride=8)] for s in range(8)]
        )

    cer, cei, cor, coi = (gathered(j) for j in range(4))
    total = jnp.concatenate([jnp.broadcast_to(v, (K, 1)) for v in totals], axis=0)
    base = cer[:, :1] * (1.0 / N) - total
    scale, edge = 2.0 / N, 1.0 / N
    ce = jnp.concatenate(
        [jnp.where(lane == 0, 0.0, cer * scale), cei * jnp.where(lane == 0, edge, scale)], axis=1
    )
    co = jnp.concatenate([cor * scale, coi * scale], axis=1)
    c_it.wait()
    u = mm3(ce, it[0], it[1])
    v = mm3(co, it[2], it[3])
    anneal = 4.0 / math.sqrt(R * N)
    low, high = anneal * (base + (u + v)), anneal * (base + (u - v))
    sc[:, :H] = low
    sc[:, H:] = high
    top = jnp.max(jnp.maximum(low, high), axis=1, keepdims=True)
    top = functools.reduce(jnp.maximum, [top[t * K : t * K + K] for t in range(T)])
    top_rows = jnp.concatenate([top] * T, axis=0)
    low, high = jnp.exp(low - top_rows), jnp.exp(high - top_rows)
    mass = jnp.sum(low + high, axis=1, keepdims=True)
    local = top + jnp.log(functools.reduce(jnp.add, [mass[t * K : t * K + K] for t in range(T)]))
    diagonal = lax.broadcasted_iota(jnp.int32, (K, LANES), 0) == lax.broadcasted_iota(
        jnp.int32, (K, LANES), 1
    )
    lsx[x] = jnp.sum(jnp.where(diagonal, local, 0.0), axis=0, keepdims=True)

    pl.semaphore_wait(barrier, len(peers))
    x_copies = []
    for d in range(1, nx):
        x_copies.append(
            pltpu.make_async_remote_copy(
                lsx.at[x], lsx.at[x], xs.at[d - 1], xr.at[d - 1],
                device_id=(dp, z * nx + (x + d) % nx), device_id_type=MESH,
            )
        )
        x_copies[-1].start()

    pe = mm3(low + high, ft[0], ft[1])
    po = mm3(low - high, ft[2], ft[3])

    for copy in x_copies:
        copy.wait_recv()
    lsz[z] = lse_of([lsx[i] for i in range(nx)])
    z_copies = []
    for d in sorted(range(1, nz), key=lambda d: -min(d, nz - d)):
        z_copies.append(
            pltpu.make_async_remote_copy(
                lsz.at[z], lsz.at[z], zs.at[d - 1], zr.at[d - 1],
                device_id=(dp, ((z + d) % nz) * nx + x), device_id_type=MESH,
            )
        )
        z_copies[-1].start()
    for copy in z_copies:
        copy.wait_recv()
    lse_row = lse_of([lsz[i] for i in range(nz)])
    lse = jnp.sum(jnp.where(diagonal, lse_row, 0.0), axis=1, keepdims=True)
    factor = jnp.exp(top - lse)
    factor_rows = jnp.concatenate([factor] * T, axis=0)
    pe, po = pe * factor_rows, po * factor_rows
    re, im = pe[:, :LANES], pe[:, LANES:]
    spectra = (
        re,
        jnp.where(lane == 0, 0.0, im),
        jnp.where(lane == 0, im, re),
        po[:, :LANES],
        po[:, LANES:],
    )
    for t in range(T):
        for j in range(5):
            for k in range(K):
                n = t * K + k
                pb[t, j, k] = jnp.broadcast_to(spectra[j][n : n + 1], (8, LANES))
    mass = mass * factor_rows
    weights = [jnp.sum(mass[t * K : t * K + K], axis=0, keepdims=True) for t in range(T)]
    weight_tile = jnp.concatenate(
        [jnp.broadcast_to(w, (8 // T, LANES)) for w in weights], axis=0
    )

    def back(owner):
        tiles = [None] * body
        for k in range(K):
            ps = [[pb[t, j, k] for j in range(5)] for t in range(T)]
            for c in range(chunks):
                rows = pl.ds(pl.multiple_of(owner * share + 8 * c, 8), 8)
                er, ei, o_r, oi = (X[k, j, rows] for j in range(4))
                for t in range(T):
                    pr, pb_, pc, qr, qi = ps[t]
                    terms = (er * pr + ei * pb_, ei * pc - er * pb_, o_r * qr + oi * qi, oi * qr - o_r * qi)
                    for j in range(4):
                        n = (t * 4 + j) * chunks + c
                        tiles[n] = terms[j] if k == 0 else tiles[n] + terms[j]
        return tiles

    order = sorted(range(1, ny), key=lambda d: -min(d, ny - d)) + [0]

    def to_core(d):
        return pltpu.make_async_remote_copy(
            sa.at[d], ra.at[d], as_.at[d], ar.at[d],
            device_id=(y * 2 + 1 - core, rot), device_id_type=MESH,
        )

    def to_chip(d):
        return pltpu.make_async_remote_copy(
            sb.at[d - 1], rb.at[d - 1], bs.at[d - 1], br.at[d - 1],
            device_id=(((y + d) % ny) * 2 + core, rot), device_id_type=MESH,
        )

    for d in order:
        for n, tile in enumerate(back(((y + d) % ny) * 2 + 1 - core)):
            sa[d, n] = tile
        sa[d, body] = weight_tile
        to_core(d).start()
    for d in order:
        tiles = back(((y + d) % ny) * 2 + core) + [weight_tile]
        to_core(d).wait_recv()
        tiles = [tile + ra[d, n] for n, tile in enumerate(tiles)]
        if d:
            for n, tile in enumerate(tiles):
                sb[d - 1, n] = tile
            to_chip(d).start()

    scores = sc[...] - jnp.concatenate([lse] * T, axis=0)
    for t in range(T):
        for q in range(N // LANES):
            logp[pl.ds(q * T + t, K, stride=T * N // LANES)] = scores[
                t * K : t * K + K, q * LANES : (q + 1) * LANES
            ]

    for d in order[:-1]:
        to_chip(d).wait_recv()
        tiles = [tile + rb[d - 1, n] for n, tile in enumerate(tiles)]
    parts = []
    for j in range(4):
        parts.append(
            jnp.concatenate(
                [tiles[(t * 4 + j) * chunks + c] for t in range(T) for c in range(chunks)], axis=0
            )
        )
    lane = lax.broadcasted_iota(jnp.int32, parts[0].shape, 1)
    ends = jnp.where(lane == 0, edge, scale)
    u = mm3(jnp.concatenate([parts[0] * ends, parts[1] * ends], axis=1), it[0], it[1])
    v = mm3(jnp.concatenate([parts[2] * scale, parts[3] * scale], axis=1), it[2], it[3])
    mine = pl.ds(pl.multiple_of(dp * share, 8), share)
    for t in range(T):
        rows = slice(t * share, (t + 1) * share)
        weight = tiles[body][t * (8 // T) : t * (8 // T) + 1, :1] + 1.0
        new[t, :, :H] = (u[rows] + v[rows] + sl[t, mine, :H]) / weight
        new[t, :, H:] = (u[rows] - v[rows] + sl[t, mine, H:]) / weight

    for copy in x_copies + z_copies:
        copy.wait_send()
    for d in order:
        to_core(d).wait_send()
    for d in order[:-1]:
        to_chip(d).wait_send()


def on_device(nx, frames, slices):
    K, R, N = frames.shape
    T = slices.shape[0]
    ny, nz = lax.axis_size("dp") // 2, lax.axis_size("rot") // nx
    share = R // (2 * ny)
    body = T * 4 * (share // 8)
    forward, inverse = packed_tables(N)
    anywhere = pl.BlockSpec(memory_space=pl.ANY)
    vmem = pl.BlockSpec(memory_space=pltpu.VMEM)
    dma = pltpu.SemaphoreType.DMA
    hops = max(nz - 1, 1)
    steps = max(ny - 1, 1)
    logp, new = pl.pallas_call(
        functools.partial(kernel, nx),
        out_shape=(
            jax.ShapeDtypeStruct((K * T * N // LANES, LANES), F32),
            jax.ShapeDtypeStruct((T, share, N), F32),
        ),
        in_specs=[anywhere] * 4,
        out_specs=(vmem, vmem),
        scratch_shapes=[
            pltpu.VMEM((K, R, N), jnp.int32),
            pltpu.VMEM((T, R, N), F32),
            pltpu.VMEM((4, N // 2, N // 2), BF16),
            pltpu.VMEM((4, N // 2, N // 2), BF16),
            pltpu.VMEM((K, 4, R, LANES), F32),
            pltpu.VMEM((T, 5, R, LANES), F32),
            pltpu.VMEM((4, T * K * 8, LANES), F32),
            pltpu.VMEM((T, 5, K, 8, LANES), F32),
            pltpu.VMEM((T * K, N), F32),
            pltpu.VMEM((nx, 1, LANES), F32),
            pltpu.VMEM((nz, 1, LANES), F32),
            pltpu.VMEM((ny, body + 1, 8, LANES), F32),
            pltpu.VMEM((ny, body + 1, 8, LANES), F32),
            pltpu.VMEM((steps, body + 1, 8, LANES), F32),
            pltpu.VMEM((steps, body + 1, 8, LANES), F32),
            dma((K,)),
            dma((3,)),
            dma((nx - 1,)),
            dma((nx - 1,)),
            dma((hops,)),
            dma((hops,)),
            dma((ny,)),
            dma((ny,)),
            dma((steps,)),
            dma((steps,)),
        ],
        compiler_params=pltpu.CompilerParams(
            collective_id=0, has_side_effects=True, vmem_limit_bytes=67_043_328
        ),
    )(frames, slices, forward, inverse)
    log_resp = logp.reshape(K, N // LANES, T, LANES).transpose(0, 2, 1, 3).reshape(K, T, N)
    return log_resp, new


def solution(mesh, nx=4):
    in_specs = (P("dp", None, None), P("rot", None, None))
    out_specs = (P("dp", "rot", None), P("rot", "dp", None))
    return jax.shard_map(
        functools.partial(on_device, nx),
        mesh=mesh, in_specs=in_specs, out_specs=out_specs, check_vma=False,
    )
```

profile of v0, /device:TPU:1, one launch (start us, length us, event | category | flops | bytes accessed | tf_op | source)
XLA Modules:
  0.0 42.6 jit_solution(15572387010619844340)
XLA Ops:
  0.6 39.0 %shard_map.59 = (f32[128,128]{1,0:T(8,128)}, f32[2,16,512]{2,1,0:T(8,128)}) custom-call(s32[16,128,512]{2,1,0:T(8,128)} %frames.1, f32[2,128,512]{2,1,0:T(8,128)} %slices.1, bf16[4,256,256]{2,1,0:T(8,128)(2,1)} %constant.4.clone.ftab_hbm, bf16[4,256,256]{2,1,0:T(8,128)(2,1)} %constant.5.clone.itab_hbm), custom_call_target="tpu_custom_call" | custom-call | tf_op jit(solution)/shard_map/pallas_call | solution.py:305
  39.6 1.5 %copy.9 = f32[16,2,512]{2,1,0:T(2,128)} copy(f32[16,2,512]{2,1,0:T(2,128)} %bitcast.5) | data formatting | bytes 131072
  41.1 1.5 %copy.10 = f32[2,16,512]{2,1,0:T(8,128)} copy(f32[2,16,512]{2,1,0:T(8,128)} %get-tuple-element.9) | data formatting | bytes 131072
where the time goes:
time: 42.8 us; the launch traced here: 42.6 us
  Pallas kernels  39 us (91%)
  local copies, waits for them, and re-layouts  2.95 us (7%)
  between operations  0.64 us (1%)
    pallas_call x1, Pallas kernels, on_device(): pl.pallas_call(functools.partial(kernel, nx), out_shape=(jax.ShapeDtypeSt...  39 us
    unnamed x2, local copies, waits for them, and re-layouts  2.95 us

commit v1 on v0

--- a/solution.py
+++ b/solution.py
@@ -12,6 +12,7 @@
 F32, BF16 = jnp.float32, jnp.bfloat16
 MESH = pl.DeviceIdType.MESH
 LANES = 128
+GROUP = 4
 
 
 def packed_tables(angles):
@@ -44,6 +45,20 @@
     return mm(xh, high) + mm(xl, high) + mm(xh, low)
 
 
+def three(re, im, first):
+    if first is None:
+        return re, re + im, re - im
+    return re, jnp.where(first, re, re + im), jnp.where(first, im, re - im)
+
+
+def joined(sums, first):
+    one, two, last = sums
+    re, im = one - last, one - two
+    if first is None:
+        return re, im
+    return jnp.where(first, two, re), jnp.where(first, last, im)
+
+
 def lse_of(rows):
     top = functools.reduce(jnp.maximum, rows)
     return top + jnp.log(functools.reduce(jnp.add, [jnp.exp(r - top) for r in rows]))
@@ -69,9 +84,14 @@
     c_it = pltpu.make_async_copy(itab_hbm, it, msem.at[2])
     c_sl.start()
     c_ft.start()
-    for k in range(K):
-        pltpu.make_async_copy(frames.at[k], fr.at[k], fsem.at[k]).start()
-    c_it.start()
+
+    def group_copy(g):
+        part = pl.ds(g * GROUP, GROUP)
+        return pltpu.make_async_copy(frames.at[part], fr.at[part], fsem.at[g])
+
+    @pl.loop(0, K // GROUP)
+    def _(g):
+        group_copy(g).start()
 
     barrier = pltpu.get_barrier_semaphore()
     peers = [(dp, z * nx + (x + d) % nx) for d in range(1, nx)]
@@ -83,7 +103,8 @@
 
     c_sl.wait()
     c_ft.wait()
-    lane = lax.broadcasted_iota(jnp.int32, (R, LANES), 1)
+    c_it.start()
+    first = lax.broadcasted_iota(jnp.int32, (R, LANES), 1) == 0
     totals = []
     for t in range(T):
         values = sl[t]
@@ -94,36 +115,34 @@
         el = (even - eh.astype(F32) - em.astype(F32)).astype(BF16)
         ye = mm(eh, ft[0]) + mm(em, ft[0]) + mm(el, ft[0]) + mm(eh, ft[1])
         yo = mm3(odd, ft[2], ft[3])
-        re, im = ye[:, :LANES], ye[:, LANES:]
-        Y[t, 0] = re
-        Y[t, 1] = jnp.where(lane == 0, 0.0, im)
-        Y[t, 2] = jnp.where(lane == 0, im, re)
-        Y[t, 3] = yo[:, :LANES]
-        Y[t, 4] = yo[:, LANES:]
-
-    @pl.loop(0, K)
-    def _(k):
-        pltpu.make_async_copy(frames.at[k], fr.at[k], fsem.at[k]).wait()
-        left, right = fr[k, :, :H], fr[k, :, H:]
-        xe = mm((left + right).astype(F32).astype(BF16), ft[0])
-        xo = mm((left - right).astype(F32).astype(BF16), ft[2])
-        X[k, 0] = xe[:, :LANES]
-        X[k, 1] = xe[:, LANES:]
-        X[k, 2] = xo[:, :LANES]
-        X[k, 3] = xo[:, LANES:]
-        sums = [None] * (4 * T)
-        for c in range(R // 8):
-            rows = slice(8 * c, 8 * c + 8)
-            er, ei, o_r, oi = (X[k, j, rows] for j in range(4))
+        pairs = three(ye[:, :LANES], ye[:, LANES:], first)
+        pairs += three(yo[:, :LANES], yo[:, LANES:], None)
+        for j in range(6):
+            Y[t, j] = pairs[j]
+
+    @pl.loop(0, K // GROUP)
+    def _(g):
+        group_copy(g).wait()
+        part = pl.ds(g * GROUP, GROUP)
+        left = fr[part, :, :H].astype(F32).astype(BF16).reshape(GROUP * R, H)
+        right = fr[part, :, H:].astype(F32).astype(BF16).reshape(GROUP * R, H)
+        outs = mm(left + right, ft[0]), mm(left - right, ft[2])
+        for i in range(GROUP):
+            k = g * GROUP + i
+            sums = [None] * (6 * T)
+            for c in range(R // 8):
+                rows = slice(8 * c, 8 * c + 8)
+                for half, out in enumerate(outs):
+                    tile = out[i * R + 8 * c : i * R + 8 * c + 8]
+                    re, im = tile[:, :LANES], tile[:, LANES:]
+                    for j, value in zip(range(3 * half, 3 * half + 3), (re + im, re, im)):
+                        X[k, j, rows] = value
+                        for t in range(T):
+                            n, term = t * 6 + j, value * Y[t, j, rows]
+                            sums[n] = term if c == 0 else sums[n] + term
             for t in range(T):
-                yr, yb, yc, zr_, zi = (Y[t, j, rows] for j in range(5))
-                terms = (er * yr + ei * yb, ei * yc - er * yb, o_r * zr_ + oi * zi, oi * zr_ - o_r * zi)
-                for j in range(4):
-                    n = 4 * t + j
-                    sums[n] = terms[j] if c == 0 else sums[n] + terms[j]
-        for t in range(T):
-            for j in range(4):
-                acc[j, pl.ds(pl.multiple_of((t * K + k) * 8, 8), 8)] = sums[4 * t + j]
+                for j in range(6):
+                    acc[j, pl.ds(pl.multiple_of((t * K + k) * 8, 8), 8)] = sums[t * 6 + j]
 
     rows = T * K
     lane = lax.broadcasted_iota(jnp.int32, (rows, LANES), 1)
@@ -133,7 +152,9 @@
             jnp.add, [acc[j, pl.ds(s, rows, stride=8)] for s in range(8)]
         )
 
-    cer, cei, cor, coi = (gathered(j) for j in range(4))
+    gathers = [gathered(j) for j in range(6)]
+    cer, cei = joined(gathers[:3], lane == 0)
+    cor, coi = joined(gathers[3:], None)
     total = jnp.concatenate([jnp.broadcast_to(v, (K, 1)) for v in totals], axis=0)
     base = cer[:, :1] * (1.0 / N) - total
     scale, edge = 2.0 / N, 1.0 / N
@@ -192,38 +213,35 @@
     factor = jnp.exp(top - lse)
     factor_rows = jnp.concatenate([factor] * T, axis=0)
     pe, po = pe * factor_rows, po * factor_rows
-    re, im = pe[:, :LANES], pe[:, LANES:]
-    spectra = (
-        re,
-        jnp.where(lane == 0, 0.0, im),
-        jnp.where(lane == 0, im, re),
-        po[:, :LANES],
-        po[:, LANES:],
-    )
-    for t in range(T):
-        for j in range(5):
-            for k in range(K):
-                n = t * K + k
-                pb[t, j, k] = jnp.broadcast_to(spectra[j][n : n + 1], (8, LANES))
+    spectra = three(pe[:, :LANES], pe[:, LANES:], lane == 0)
+    spectra += three(po[:, :LANES], po[:, LANES:], None)
+    for j in range(6):
+        pb[j] = spectra[j]
     mass = mass * factor_rows
     weights = [jnp.sum(mass[t * K : t * K + K], axis=0, keepdims=True) for t in range(T)]
     weight_tile = jnp.concatenate(
         [jnp.broadcast_to(w, (8 // T, LANES)) for w in weights], axis=0
     )
 
+    first = lax.broadcasted_iota(jnp.int32, (8, LANES), 1) == 0
+
     def back(owner):
-        tiles = [None] * body
+        sums = [[[None] * 6 for c in range(chunks)] for t in range(T)]
         for k in range(K):
-            ps = [[pb[t, j, k] for j in range(5)] for t in range(T)]
+            ps = [[pb[j, pl.ds(t * K + k, 8, stride=0)] for j in range(6)] for t in range(T)]
             for c in range(chunks):
                 rows = pl.ds(pl.multiple_of(owner * share + 8 * c, 8), 8)
-                er, ei, o_r, oi = (X[k, j, rows] for j in range(4))
-                for t in range(T):
-                    pr, pb_, pc, qr, qi = ps[t]
-                    terms = (er * pr + ei * pb_, ei * pc - er * pb_, o_r * qr + oi * qi, oi * qr - o_r * qi)
-                    for j in range(4):
-                        n = (t * 4 + j) * chunks + c
-                        tiles[n] = terms[j] if k == 0 else tiles[n] + terms[j]
+                for j in range(6):
+                    x_ = X[k, j, rows]
+                    for t in range(T):
+                        term = x_ * ps[t][j]
+                        sums[t][c][j] = term if k == 0 else sums[t][c][j] + term
+        tiles = [None] * body
+        for t in range(T):
+            for c in range(chunks):
+                parts = joined(sums[t][c][:3], first) + joined(sums[t][c][3:], None)
+                for j in range(4):
+                    tiles[(t * 4 + j) * chunks + c] = parts[j]
         return tiles
 
     order = sorted(range(1, ny), key=lambda d: -min(d, ny - d)) + [0]
@@ -290,6 +308,17 @@
         to_chip(d).wait_send()
 
 
+def hand_over(logp, new, logp_out, new_out, sem):
+    copies = [
+        pltpu.make_async_copy(logp, logp_out, sem.at[0]),
+        pltpu.make_async_copy(new, new_out, sem.at[1]),
+    ]
+    for copy in copies:
+        copy.start()
+    for copy in copies:
+        copy.wait()
+
+
 def on_device(nx, frames, slices):
     K, R, N = frames.shape
     T = slices.shape[0]
@@ -297,7 +326,7 @@
     share = R // (2 * ny)
     body = T * 4 * (share // 8)
     forward, inverse = packed_tables(N)
-    anywhere = pl.BlockSpec(memory_space=pl.ANY)
+    hbm = pl.BlockSpec(memory_space=pltpu.HBM)
     vmem = pl.BlockSpec(memory_space=pltpu.VMEM)
     dma = pltpu.SemaphoreType.DMA
     hops = max(nz - 1, 1)
@@ -308,17 +337,17 @@
             jax.ShapeDtypeStruct((K * T * N // LANES, LANES), F32),
             jax.ShapeDtypeStruct((T, share, N), F32),
         ),
-        in_specs=[anywhere] * 4,
+        in_specs=[hbm] * 4,
         out_specs=(vmem, vmem),
         scratch_shapes=[
             pltpu.VMEM((K, R, N), jnp.int32),
             pltpu.VMEM((T, R, N), F32),
             pltpu.VMEM((4, N // 2, N // 2), BF16),
             pltpu.VMEM((4, N // 2, N // 2), BF16),
-            pltpu.VMEM((K, 4, R, LANES), F32),
-            pltpu.VMEM((T, 5, R, LANES), F32),
-            pltpu.VMEM((4, T * K * 8, LANES), F32),
-            pltpu.VMEM((T, 5, K, 8, LANES), F32),
+            pltpu.VMEM((K, 6, R, LANES), F32),
+            pltpu.VMEM((T, 6, R, LANES), F32),
+            pltpu.VMEM((6, 8 * T * K, LANES), F32),
+            pltpu.VMEM((6, T * K, LANES), F32),
             pltpu.VMEM((T * K, N), F32),
             pltpu.VMEM((nx, 1, LANES), F32),
             pltpu.VMEM((nz, 1, LANES), F32),
@@ -326,7 +355,7 @@
             pltpu.VMEM((ny, body + 1, 8, LANES), F32),
             pltpu.VMEM((steps, body + 1, 8, LANES), F32),
             pltpu.VMEM((steps, body + 1, 8, LANES), F32),
-            dma((K,)),
+            dma((K // GROUP,)),
             dma((3,)),
             dma((nx - 1,)),
             dma((nx - 1,)),
@@ -338,9 +367,20 @@
             dma((steps,)),
         ],
         compiler_params=pltpu.CompilerParams(
-            collective_id=0, has_side_effects=True, vmem_limit_bytes=67_043_328
+            collective_id=0, has_side_effects=True, vmem_limit_bytes=32 << 20
         ),
-    )(frames, slices, forward, inverse)
+    )(*(pltpu.with_memory_space_constraint(v, pltpu.HBM) for v in (frames, slices, jnp.asarray(forward), jnp.asarray(inverse))))
+    logp, new = pl.pallas_call(
+        hand_over,
+        out_shape=(
+            jax.ShapeDtypeStruct(logp.shape, F32),
+            jax.ShapeDtypeStruct(new.shape, F32),
+        ),
+        in_specs=[vmem, vmem],
+        out_specs=(hbm, hbm),
+        scratch_shapes=[dma((2,))],
+        compiler_params=pltpu.CompilerParams(vmem_limit_bytes=1 << 20),
+    )(logp, new)
     log_resp = logp.reshape(K, N // LANES, T, LANES).transpose(0, 2, 1, 3).reshape(K, T, N)
     return log_resp, new
 

time: 42.8 us -> 36.3 us (0.85)
  Pallas kernels: 39 us -> 35.6 us
  local copies, waits for them, and re-layouts: 2.95 us -> 0 us
    pallas_call x1, Pallas kernels: 39 us -> 34.9 us  [on_device(): pl.pallas_call(functools.partial(kernel, nx), out_shape=(jax.ShapeDtypeSt...]
    unnamed x2 -> x0, local copies, waits for them, and re-layouts: 2.95 us -> none
    pallas_call x0 -> x1, Pallas kernels: none -> 0.67 us  [on_device(): pl.pallas_call(hand_over, out_shape=(jax.ShapeDtypeStruct(logp.shape, F32...]
where the time goes in v1:
time: 36.3 us; the launch traced here: 36.2 us
  Pallas kernels  35.6 us (98%)
  between operations  0.64 us (2%)
    pallas_call x1, Pallas kernels, on_device(): pl.pallas_call(functools.partial(kernel, nx), out_shape=(jax.ShapeDtypeSt...  34.9 us

profile of v1, /device:TPU:1, one launch (start us, length us, event | category | flops | bytes accessed | tf_op | source)
XLA Modules:
  0.0 36.2 jit_solution(2150808945616384408)
XLA Ops:
  0.6 34.9 %shard_map.59 = (f32[128,128]{1,0:T(8,128)S(1)}, f32[2,16,512]{2,1,0:T(8,128)S(1)}) custom-call(s32[16,128,512]{2,1,0:T(8,128)} %frames.1, f32[2,128,512]{2,1,0:T(8,128)} %slices.1, bf16[4,256,256]{2,1,0:T(8,128)(2,1)} %constant.4.clone.ftab_hbm, bf16[4,256,256]{2,1,0:T(8,128)(2,1)} %constant.5.clone.itab_hbm), custom_call_target="tpu_custom_call" | custom-call | tf_op jit(solution)/shard_map/pallas_call | solution.py:334
  35.6 0.7 %shard_map.60 = (f32[128,128]{1,0:T(8,128)}, f32[2,16,512]{2,1,0:T(8,128)}) custom-call(f32[128,128]{1,0:T(8,128)S(1)} %get-tuple-element.6.logp, f32[2,16,512]{2,1,0:T(8,128)S(1)} %get-tuple-element.7.new), custom_call_target="tpu_custom_call" | custom-call | tf_op jit(solution)/shard_map/pallas_call | solution.py:373

commit v2 on v1

--- a/solution.py
+++ b/solution.py
@@ -41,8 +41,16 @@
 
 
 def mm3(x, high, low):
-    xh, xl = split(x)
-    return mm(xh, high) + mm(xl, high) + mm(xh, low)
+    return mm_parts(split(x), high, low)
+
+
+def mm_parts(parts, high, low):
+    rows = parts[0].shape[0]
+    stacked = mm(jnp.concatenate(parts, axis=0), high)
+    total = mm(parts[0], low)
+    for i in reversed(range(len(parts))):
+        total = total + stacked[i * rows : (i + 1) * rows]
+    return total
 
 
 def three(re, im, first):
@@ -59,15 +67,10 @@
     return jnp.where(first, two, re), jnp.where(first, last, im)
 
 
-def lse_of(rows):
-    top = functools.reduce(jnp.maximum, rows)
-    return top + jnp.log(functools.reduce(jnp.add, [jnp.exp(r - top) for r in rows]))
-
-
 def kernel(
     nx, frames, slices, ftab_hbm, itab_hbm, logp, new,
-    fr, sl, ft, it, X, Y, acc, pb, sc, lsx, lsz, sa, ra, sb, rb,
-    fsem, msem, xs, xr, zs, zr, as_, ar, bs, br,
+    fr, sl, ft, it, X, Y, acc, pb, sc, ls, fin, wt, sa, ra, sb, rb,
+    fsem, msem, ls_sem, fin_sem, wt_sem, as_, ar, bs, br,
 ):
     K, R, N = fr.shape
     T, H = sl.shape[0], N // 2
@@ -76,34 +79,53 @@
     y, core = dp // 2, dp % 2
     z, x = rot // nx, rot % nx
     share = R // (2 * ny)
-    chunks = share // 8
-    body = T * 4 * chunks
+    chunks, half = share // 8, T * 4
+    body = half * chunks
 
     c_ft = pltpu.make_async_copy(ftab_hbm, ft, msem.at[0])
     c_sl = pltpu.make_async_copy(slices, sl, msem.at[1])
     c_it = pltpu.make_async_copy(itab_hbm, it, msem.at[2])
-    c_sl.start()
-    c_ft.start()
+    for i in range(4):
+        for t in range(T):
+            part = pl.ds(i * R // 4, R // 4)
+            pltpu.make_async_copy(slices.at[t, part], sl.at[t, part], msem.at[1]).start()
+        pltpu.make_async_copy(ftab_hbm.at[i], ft.at[i], msem.at[0]).start()
 
     def group_copy(g):
         part = pl.ds(g * GROUP, GROUP)
         return pltpu.make_async_copy(frames.at[part], fr.at[part], fsem.at[g])
 
-    @pl.loop(0, K // GROUP)
-    def _(g):
-        group_copy(g).start()
-
     barrier = pltpu.get_barrier_semaphore()
-    peers = [(dp, z * nx + (x + d) % nx) for d in range(1, nx)]
-    peers += [(dp, ((z + d) % nz) * nx + x) for d in range(1, nz)]
-    peers += [(y * 2 + 1 - core, rot)]
-    peers += [(((y + d) % ny) * 2 + core, rot) for d in range(1, ny)]
-    for peer in peers:
+    low_z = nz // 2
+    lower = z < low_z
+    steps = [(i, j) for i in range(low_z) for j in range(nx)]
+    steps.sort(key=lambda s: -(min(s[0], low_z - s[0]) + min(s[1], nx - s[1])))
+
+    def at(i, j, upper=0):
+        return dp, ((z + i) % low_z + upper * low_z) * nx + (x + j) % nx
+
+    mine = [at(i, j) for i, j in steps if i or j]
+    opposite = [at(i, j, 1) for i, j in steps]
+    family = [((dp + d) % (2 * ny), rot) for d in range(1, 2 * ny)]
+    def signal(peer):
         pl.semaphore_signal(barrier, inc=1, device_id=peer, device_id_type=MESH)
+
+    @pl.when(lower)
+    def _():
+        for peer in opposite + mine:
+            signal(peer)
+
+    for peer in family:
+        signal(peer)
+
+    @pl.loop(0, K)
+    def _(k):
+        pltpu.make_async_copy(frames.at[k], fr.at[k], fsem.at[k // GROUP]).start()
+
+    c_it.start()
 
     c_sl.wait()
     c_ft.wait()
-    c_it.start()
     first = lax.broadcasted_iota(jnp.int32, (R, LANES), 1) == 0
     totals = []
     for t in range(T):
@@ -113,7 +135,7 @@
         even, odd = logs[:, :H] + logs[:, H:], logs[:, :H] - logs[:, H:]
         eh, em = split(even)
         el = (even - eh.astype(F32) - em.astype(F32)).astype(BF16)
-        ye = mm(eh, ft[0]) + mm(em, ft[0]) + mm(el, ft[0]) + mm(eh, ft[1])
+        ye = mm_parts((eh, em, el), ft[0], ft[1])
         yo = mm3(odd, ft[2], ft[3])
         pairs = three(ye[:, :LANES], ye[:, LANES:], first)
         pairs += three(yo[:, :LANES], yo[:, LANES:], None)
@@ -178,37 +200,54 @@
     diagonal = lax.broadcasted_iota(jnp.int32, (K, LANES), 0) == lax.broadcasted_iota(
         jnp.int32, (K, LANES), 1
     )
-    lsx[x] = jnp.sum(jnp.where(diagonal, local, 0.0), axis=0, keepdims=True)
-
-    pl.semaphore_wait(barrier, len(peers))
-    x_copies = []
-    for d in range(1, nx):
-        x_copies.append(
-            pltpu.make_async_remote_copy(
-                lsx.at[x], lsx.at[x], xs.at[d - 1], xr.at[d - 1],
-                device_id=(dp, z * nx + (x + d) % nx), device_id_type=MESH,
-            )
+    ls[rot] = jnp.sum(jnp.where(diagonal, local, 0.0), axis=0, keepdims=True)
+
+    def tell(peer):
+        pltpu.make_async_remote_copy(
+            ls.at[rot], ls.at[rot], ls_sem.at[0], ls_sem.at[1],
+            device_id=peer, device_id_type=MESH,
+        ).start()
+
+    def wait_rows(ref, n, sem):
+        rows = ref.at[pl.ds(0, n)]
+        pltpu.make_async_copy(rows, rows, sem).wait()
+
+    def answer():
+        return pltpu.make_async_remote_copy(
+            fin.at[0], fin.at[0], fin_sem.at[0], fin_sem.at[1],
+            device_id=at(0, 0, 1), device_id_type=MESH,
         )
-        x_copies[-1].start()
+
+    everyone = nz * nx
+
+    @pl.when(lower)
+    def _():
+        pl.semaphore_wait(barrier, len(mine) + len(family))
+
+    @pl.when(jnp.logical_not(lower))
+    def _():
+        pl.semaphore_wait(barrier, len(opposite) + len(family))
+        tell(at(0, 0))
+
+    for peer in mine:
+        tell(peer)
 
     pe = mm3(low + high, ft[0], ft[1])
     po = mm3(low - high, ft[2], ft[3])
 
-    for copy in x_copies:
-        copy.wait_recv()
-    lsz[z] = lse_of([lsx[i] for i in range(nx)])
-    z_copies = []
-    for d in sorted(range(1, nz), key=lambda d: -min(d, nz - d)):
-        z_copies.append(
-            pltpu.make_async_remote_copy(
-                lsz.at[z], lsz.at[z], zs.at[d - 1], zr.at[d - 1],
-                device_id=(dp, ((z + d) % nz) * nx + x), device_id_type=MESH,
-            )
-        )
-        z_copies[-1].start()
-    for copy in z_copies:
-        copy.wait_recv()
-    lse_row = lse_of([lsz[i] for i in range(nz)])
+    @pl.when(lower)
+    def _():
+        wait_rows(ls, everyone - 1, ls_sem.at[1])
+        each = ls[...]
+        peak = jnp.max(each, axis=0)
+        fin[0] = peak + jnp.log(jnp.sum(jnp.exp(each - peak), axis=0))
+        answer().start()
+
+    @pl.when(jnp.logical_not(lower))
+    def _():
+        answer().wait_recv()
+
+    lse_row = fin[0]
     lse = jnp.sum(jnp.where(diagonal, lse_row, 0.0), axis=1, keepdims=True)
     factor = jnp.exp(top - lse)
     factor_rows = jnp.concatenate([factor] * T, axis=0)
@@ -219,9 +258,8 @@
         pb[j] = spectra[j]
     mass = mass * factor_rows
     weights = [jnp.sum(mass[t * K : t * K + K], axis=0, keepdims=True) for t in range(T)]
-    weight_tile = jnp.concatenate(
-        [jnp.broadcast_to(w, (8 // T, LANES)) for w in weights], axis=0
-    )
+    lane = lax.broadcasted_iota(jnp.int32, (1, LANES), 1)
+    wt[dp] = functools.reduce(jnp.add, [jnp.where(lane == t, weights[t], 0.0) for t in range(T)])
 
     first = lax.broadcasted_iota(jnp.int32, (8, LANES), 1) == 0
 
@@ -241,10 +279,10 @@
             for c in range(chunks):
                 parts = joined(sums[t][c][:3], first) + joined(sums[t][c][3:], None)
                 for j in range(4):
-                    tiles[(t * 4 + j) * chunks + c] = parts[j]
+                    tiles[c * half + t * 4 + j] = parts[j]
         return tiles
 
-    order = sorted(range(1, ny), key=lambda d: -min(d, ny - d)) + [0]
+    order = (2, 1, 3, 0)
 
     def to_core(d):
         return pltpu.make_async_remote_copy(
@@ -252,25 +290,47 @@
             device_id=(y * 2 + 1 - core, rot), device_id_type=MESH,
         )
 
-    def to_chip(d):
+    def to_chip(n):
         return pltpu.make_async_remote_copy(
-            sb.at[d - 1], rb.at[d - 1], bs.at[d - 1], br.at[d - 1],
-            device_id=(((y + d) % ny) * 2 + core, rot), device_id_type=MESH,
+            sb.at[n], rb.at[n], bs.at[n], br.at[n],
+            device_id=((y + (1 if n < 3 else ny - 1)) % ny * 2 + core, rot), device_id_type=MESH,
         )
 
+    def send(n, tiles):
+        for i, tile in enumerate(tiles):
+            sb[n, i] = tile
+        to_chip(n).start()
+
+    def plus(tiles, n):
+        to_chip(n).wait_recv()
+        return [tile + rb[n, i] for i, tile in enumerate(tiles)]
+
     for d in order:
-        for n, tile in enumerate(back(((y + d) % ny) * 2 + 1 - core)):
+        for n, tile in enumerate(back((y + d) % ny * 2 + 1 - core)):
             sa[d, n] = tile
-        sa[d, body] = weight_tile
         to_core(d).start()
-    for d in order:
-        tiles = back(((y + d) % ny) * 2 + core) + [weight_tile]
+        if d == order[0]:
+            for peer in family:
+                pltpu.make_async_remote_copy(
+                    wt.at[dp], wt.at[dp], wt_sem.at[0], wt_sem.at[1],
+                    device_id=peer, device_id_type=MESH,
+                ).start()
+
+    def chip_sum(d):
+        tiles = back((y + d) % ny * 2 + core)
         to_core(d).wait_recv()
-        tiles = [tile + ra[d, n] for n, tile in enumerate(tiles)]
-        if d:
-            for n, tile in enumerate(tiles):
-                sb[d - 1, n] = tile
-            to_chip(d).start()
+        return [tile + ra[d, n] for n, tile in enumerate(tiles)]
+
+    tiles = chip_sum(2)
+    send(0, tiles[:half])
+    send(3, tiles[half:])
+    ahead = chip_sum(1)
+    send(1, ahead[half:])
+    behind = chip_sum(3)
+    send(4, behind[:half])
+    send(2, plus(ahead[:half], 0))
+    send(5, plus(behind[half:], 3))
+    tiles = chip_sum(0)
 
     scores = sc[...] - jnp.concatenate([lse] * T, axis=0)
     for t in range(T):
@@ -279,33 +339,44 @@
                 t * K : t * K + K, q * LANES : (q + 1) * LANES
             ]
 
-    for d in order[:-1]:
-        to_chip(d).wait_recv()
-        tiles = [tile + rb[d - 1, n] for n, tile in enumerate(tiles)]
+    tiles = plus(tiles[:half], 4) + plus(tiles[half:], 1)
+    tiles = plus(tiles[:half], 2) + plus(tiles[half:], 5)
+    family_rows = wt.at[pl.ds(0, len(family))]
+    pltpu.make_async_copy(family_rows, family_rows, wt_sem.at[1]).wait()
+    weight_row = jnp.sum(wt[...], axis=0) + 1.0
     parts = []
     for j in range(4):
         parts.append(
             jnp.concatenate(
-                [tiles[(t * 4 + j) * chunks + c] for t in range(T) for c in range(chunks)], axis=0
+                [tiles[c * half + t * 4 + j] for t in range(T) for c in range(chunks)], axis=0
             )
         )
     lane = lax.broadcasted_iota(jnp.int32, parts[0].shape, 1)
     ends = jnp.where(lane == 0, edge, scale)
     u = mm3(jnp.concatenate([parts[0] * ends, parts[1] * ends], axis=1), it[0], it[1])
     v = mm3(jnp.concatenate([parts[2] * scale, parts[3] * scale], axis=1), it[2], it[3])
-    mine = pl.ds(pl.multiple_of(dp * share, 8), share)
+    owned = pl.ds(pl.multiple_of(dp * share, 8), share)
     for t in range(T):
         rows = slice(t * share, (t + 1) * share)
-        weight = tiles[body][t * (8 // T) : t * (8 // T) + 1, :1] + 1.0
-        new[t, :, :H] = (u[rows] + v[rows] + sl[t, mine, :H]) / weight
-        new[t, :, H:] = (u[rows] - v[rows] + sl[t, mine, H:]) / weight
-
-    for copy in x_copies + z_copies:
-        copy.wait_send()
+        weight = weight_row[:, t : t + 1]
+        new[t, :, :H] = (u[rows] + v[rows] + sl[t, owned, :H]) / weight
+        new[t, :, H:] = (u[rows] - v[rows] + sl[t, owned, H:]) / weight
+
+    wait_rows(ls, len(mine), ls_sem.at[0])
+
+    @pl.when(lower)
+    def _():
+        answer().wait_send()
+
+    @pl.when(jnp.logical_not(lower))
+    def _():
+        wait_rows(ls, 1, ls_sem.at[0])
+
+    pltpu.make_async_copy(family_rows, family_rows, wt_sem.at[0]).wait()
     for d in order:
         to_core(d).wait_send()
-    for d in order[:-1]:
-        to_chip(d).wait_send()
+    for n in range(6):
+        to_chip(n).wait_send()
 
 
 def hand_over(logp, new, logp_out, new_out, sem):
@@ -323,14 +394,13 @@
     K, R, N = frames.shape
     T = slices.shape[0]
     ny, nz = lax.axis_size("dp") // 2, lax.axis_size("rot") // nx
+    assert ny == 4 and R // (2 * ny) == 16
     share = R // (2 * ny)
     body = T * 4 * (share // 8)
     forward, inverse = packed_tables(N)
     hbm = pl.BlockSpec(memory_space=pltpu.HBM)
     vmem = pl.BlockSpec(memory_space=pltpu.VMEM)
     dma = pltpu.SemaphoreType.DMA
-    hops = max(nz - 1, 1)
-    steps = max(ny - 1, 1)
     logp, new = pl.pallas_call(
         functools.partial(kernel, nx),
         out_shape=(
@@ -349,22 +419,22 @@
             pltpu.VMEM((6, 8 * T * K, LANES), F32),
             pltpu.VMEM((6, T * K, LANES), F32),
             pltpu.VMEM((T * K, N), F32),
-            pltpu.VMEM((nx, 1, LANES), F32),
-            pltpu.VMEM((nz, 1, LANES), F32),
-            pltpu.VMEM((ny, body + 1, 8, LANES), F32),
-            pltpu.VMEM((ny, body + 1, 8, LANES), F32),
-            pltpu.VMEM((steps, body + 1, 8, LANES), F32),
-            pltpu.VMEM((steps, body + 1, 8, LANES), F32),
+            pltpu.VMEM((nx * nz, 1, LANES), F32),
+            pltpu.VMEM((1, 1, LANES), F32),
+            pltpu.VMEM((2 * ny, 1, LANES), F32),
+            pltpu.VMEM((ny, body, 8, LANES), F32),
+            pltpu.VMEM((ny, body, 8, LANES), F32),
+            pltpu.VMEM((6, body // 2, 8, LANES), F32),
+            pltpu.VMEM((6, body // 2, 8, LANES), F32),
             dma((K // GROUP,)),
             dma((3,)),
-            dma((nx - 1,)),
-            dma((nx - 1,)),
-            dma((hops,)),
-            dma((hops,)),
+            dma((2,)),
+            dma((2,)),
+            dma((2,)),
             dma((ny,)),
             dma((ny,)),
-            dma((steps,)),
-            dma((steps,)),
+            dma((6,)),
+            dma((6,)),
         ],
         compiler_params=pltpu.CompilerParams(
             collective_id=0, has_side_effects=True, vmem_limit_bytes=32 << 20

time: 36.3 us -> 33.7 us (0.928)
  Pallas kernels: 35.6 us -> 32.9 us
    pallas_call x1, Pallas kernels: 34.9 us -> 32.3 us  [on_device(): pl.pallas_call(functools.partial(kernel, nx), out_shape=(jax.ShapeDtypeSt...]
where the time goes in v2:
time: 33.7 us; the launch traced here: 33.6 us
  Pallas kernels  32.9 us (98%)
  between operations  0.64 us (2%)
    pallas_call x1, Pallas kernels, on_device(): pl.pallas_call(functools.partial(kernel, nx), out_shape=(jax.ShapeDtypeSt...  32.3 us

profile of v2, /device:TPU:1, one launch (start us, length us, event | category | flops | bytes accessed | tf_op | source)
XLA Modules:
  0.0 33.6 jit_solution(11180001330798741401)
XLA Ops:
  0.6 32.3 %shard_map.59 = (f32[128,128]{1,0:T(8,128)S(1)}, f32[2,16,512]{2,1,0:T(8,128)S(1)}) custom-call(s32[16,128,512]{2,1,0:T(8,128)} %frames.1, f32[2,128,512]{2,1,0:T(8,128)} %slices.1, bf16[4,256,256]{2,1,0:T(8,128)(2,1)} %constant.4.clone.ftab_hbm, bf16[4,256,256]{2,1,0:T(8,128)(2,1)} %constant.5.clone.itab_hbm), custom_call_target="tpu_custom_call" | custom-call | tf_op jit(solution)/shard_map/pallas_call | solution.py:404
  32.9 0.7 %shard_map.60 = (f32[128,128]{1,0:T(8,128)}, f32[2,16,512]{2,1,0:T(8,128)}) custom-call(f32[128,128]{1,0:T(8,128)S(1)} %get-tuple-element.6.logp, f32[2,16,512]{2,1,0:T(8,128)S(1)} %get-tuple-element.7.new), custom_call_target="tpu_custom_call" | custom-call | tf_op jit(solution)/shard_map/pallas_call | solution.py:443

commit v3 on v2

--- a/solution.py
+++ b/solution.py
@@ -67,9 +67,14 @@
     return jnp.where(first, two, re), jnp.where(first, last, im)
 
 
+def lse_of_rows(rows):
+    peak = jnp.max(rows, axis=0)
+    return peak + jnp.log(jnp.sum(jnp.exp(rows - peak), axis=0))
+
+
 def kernel(
     nx, frames, slices, ftab_hbm, itab_hbm, logp, new,
-    fr, sl, ft, it, X, Y, acc, pb, sc, ls, fin, wt, sa, ra, sb, rb,
+    fr, sl, ft, it, X, Y, acc, pb, sc, ls, fin, wt, kept, sa, ra, sb, rb,
     fsem, msem, ls_sem, fin_sem, wt_sem, as_, ar, bs, br,
 ):
     K, R, N = fr.shape
@@ -204,7 +209,7 @@
 
     def tell(peer):
         pltpu.make_async_remote_copy(
-            ls.at[rot], ls.at[rot], ls_sem.at[0], ls_sem.at[1],
+            ls.at[rot], ls.at[rot], ls_sem.at[0], ls_sem.at[1 + z // low_z],
             device_id=peer, device_id_type=MESH,
         ).start()
 
@@ -237,10 +242,12 @@
 
     @pl.when(lower)
     def _():
-        wait_rows(ls, everyone - 1, ls_sem.at[1])
-        each = ls[...]
-        peak = jnp.max(each, axis=0)
-        fin[0] = peak + jnp.log(jnp.sum(jnp.exp(each - peak), axis=0))
+        wait_rows(ls, len(mine), ls_sem.at[1])
+        near_row = lse_of_rows(ls[: everyone // 2])
+        wait_rows(ls, everyone // 2, ls_sem.at[2])
+        far_row = lse_of_rows(ls[everyone // 2 :])
+        peak = jnp.maximum(near_row, far_row)
+        fin[0] = peak + jnp.log(jnp.exp(near_row - peak) + jnp.exp(far_row - peak))
         answer().start()
 
     @pl.when(jnp.logical_not(lower))
@@ -290,46 +297,68 @@
             device_id=(y * 2 + 1 - core, rot), device_id_type=MESH,
         )
 
-    def to_chip(n):
+    def to_chip(n, p):
+        piece = pl.ds(p * half // 2, half // 2)
         return pltpu.make_async_remote_copy(
-            sb.at[n], rb.at[n], bs.at[n], br.at[n],
+            sb.at[n, piece], rb.at[n, piece], bs.at[2 * n + p], br.at[2 * n + p],
             device_id=((y + (1 if n < 3 else ny - 1)) % ny * 2 + core, rot), device_id_type=MESH,
         )
 
+    def send_piece(n, p, tiles):
+        for i, tile in enumerate(tiles):
+            sb[n, p * half // 2 + i] = tile
+        to_chip(n, p).start()
+
     def send(n, tiles):
-        for i, tile in enumerate(tiles):
-            sb[n, i] = tile
-        to_chip(n).start()
+        for p in range(2):
+            send_piece(n, p, tiles[p * half // 2 : (p + 1) * half // 2])
+
+    def plus_piece(tiles, n, p):
+        to_chip(n, p).wait_recv()
+        return [tile + rb[n, p * half // 2 + i] for i, tile in enumerate(tiles)]
 
     def plus(tiles, n):
-        to_chip(n).wait_recv()
-        return [tile + rb[n, i] for i, tile in enumerate(tiles)]
-
-    for d in order:
+        return plus_piece(tiles[: half // 2], n, 0) + plus_piece(tiles[half // 2 :], n, 1)
+
+    def give(d):
         for n, tile in enumerate(back((y + d) % ny * 2 + 1 - core)):
             sa[d, n] = tile
         to_core(d).start()
-        if d == order[0]:
-            for peer in family:
-                pltpu.make_async_remote_copy(
-                    wt.at[dp], wt.at[dp], wt_sem.at[0], wt_sem.at[1],
-                    device_id=peer, device_id_type=MESH,
-                ).start()
 
     def chip_sum(d):
         tiles = back((y + d) % ny * 2 + core)
         to_core(d).wait_recv()
         return [tile + ra[d, n] for n, tile in enumerate(tiles)]
 
+    def give_on(which, ds):
+        @pl.when(core == which)
+        def _():
+            for d in ds:
+                give(d)
+
+    give(2)
+    for peer in family:
+        pltpu.make_async_remote_copy(
+            wt.at[dp], wt.at[dp], wt_sem.at[0], wt_sem.at[1],
+            device_id=peer, device_id_type=MESH,
+        ).start()
+    give_on(1, (1, 3, 0))
     tiles = chip_sum(2)
     send(0, tiles[:half])
     send(3, tiles[half:])
+    give_on(0, (1, 3, 0))
     ahead = chip_sum(1)
     send(1, ahead[half:])
+    for n in range(half):
+        kept[0, n] = ahead[n]
     behind = chip_sum(3)
     send(4, behind[:half])
-    send(2, plus(ahead[:half], 0))
-    send(5, plus(behind[half:], 3))
+    for n in range(half):
+        kept[1, n] = behind[half + n]
+    for p in range(2):
+        for i, came, goes in ((0, 0, 2), (1, 3, 5)):
+            piece = [kept[i, p * half // 2 + n] for n in range(half // 2)]
+            send_piece(goes, p, plus_piece(piece, came, p))
     tiles = chip_sum(0)
 
     scores = sc[...] - jnp.concatenate([lse] * T, axis=0)
@@ -376,7 +405,8 @@
     for d in order:
         to_core(d).wait_send()
     for n in range(6):
-        to_chip(n).wait_send()
+        for p in range(2):
+            to_chip(n, p).wait_send()
 
 
 def hand_over(logp, new, logp_out, new_out, sem):
@@ -422,19 +452,20 @@
             pltpu.VMEM((nx * nz, 1, LANES), F32),
             pltpu.VMEM((1, 1, LANES), F32),
             pltpu.VMEM((2 * ny, 1, LANES), F32),
+            pltpu.VMEM((2, body // 2, 8, LANES), F32),
             pltpu.VMEM((ny, body, 8, LANES), F32),
             pltpu.VMEM((ny, body, 8, LANES), F32),
             pltpu.VMEM((6, body // 2, 8, LANES), F32),
             pltpu.VMEM((6, body // 2, 8, LANES), F32),
             dma((K // GROUP,)),
             dma((3,)),
-            dma((2,)),
+            dma((3,)),
             dma((2,)),
             dma((2,)),
             dma((ny,)),
             dma((ny,)),
-            dma((6,)),
-            dma((6,)),
+            dma((12,)),
+            dma((12,)),
         ],
         compiler_params=pltpu.CompilerParams(
             collective_id=0, has_side_effects=True, vmem_limit_bytes=32 << 20

time: 33.7 us -> 33.7 us (level)
  no operation moved by 1% of the time
where the time goes in v3:
time: 33.7 us; the launch traced here: 33.6 us
  Pallas kernels  33 us (98%)
  between operations  0.64 us (2%)
    pallas_call x1, Pallas kernels, on_device(): pl.pallas_call(functools.partial(kernel, nx), out_shape=(jax.ShapeDtypeSt...  32.3 us

profile of v3, /device:TPU:1, one launch (start us, length us, event | category | flops | bytes accessed | tf_op | source)
XLA Modules:
  0.0 33.6 jit_solution(8144199278374744238)
XLA Ops:
  0.6 32.3 %shard_map.59 = (f32[128,128]{1,0:T(8,128)S(1)}, f32[2,16,512]{2,1,0:T(8,128)S(1)}) custom-call(s32[16,128,512]{2,1,0:T(8,128)} %frames.1, f32[2,128,512]{2,1,0:T(8,128)} %slices.1, bf16[4,256,256]{2,1,0:T(8,128)(2,1)} %constant.4.clone.ftab_hbm, bf16[4,256,256]{2,1,0:T(8,128)(2,1)} %constant.5.clone.itab_hbm), custom_call_target="tpu_custom_call" | custom-call | tf_op jit(solution)/shard_map/pallas_call | solution.py:434
  32.9 0.7 %shard_map.60 = (f32[128,128]{1,0:T(8,128)}, f32[2,16,512]{2,1,0:T(8,128)}) custom-call(f32[128,128]{1,0:T(8,128)S(1)} %get-tuple-element.6.logp, f32[2,16,512]{2,1,0:T(8,128)S(1)} %get-tuple-element.7.new), custom_call_target="tpu_custom_call" | custom-call | tf_op jit(solution)/shard_map/pallas_call | solution.py:474

commit v4 on v3

--- a/solution.py
+++ b/solution.py
@@ -27,12 +27,11 @@
     for table in (even, odd):
         high = table.astype(BF16)
         parts += [high, (table - high.astype(np.float64)).astype(BF16)]
-    forward = np.stack(parts)
-    return forward, np.ascontiguousarray(forward.transpose(0, 2, 1))
-
-
-def mm(a, b):
-    return jnp.dot(a, b, preferred_element_type=F32)
+    return np.stack(parts)[:, : half // 2]
+
+
+def mm(a, b, axis=0):
+    return lax.dot_general(a, b, (((1,), (axis,)), ((), ())), preferred_element_type=F32)
 
 
 def split(x):
@@ -40,14 +39,14 @@
     return high, (x - high.astype(F32)).astype(BF16)
 
 
-def mm3(x, high, low):
-    return mm_parts(split(x), high, low)
-
-
-def mm_parts(parts, high, low):
+def mm3(x, high, low, axis=0):
+    return mm_parts(split(x), high, low, axis)
+
+
+def mm_parts(parts, high, low, axis=0):
     rows = parts[0].shape[0]
-    stacked = mm(jnp.concatenate(parts, axis=0), high)
-    total = mm(parts[0], low)
+    stacked = mm(jnp.concatenate(parts, axis=0), high, axis)
+    total = mm(parts[0], low, axis)
     for i in reversed(range(len(parts))):
         total = total + stacked[i * rows : (i + 1) * rows]
     return total
@@ -73,8 +72,8 @@
 
 
 def kernel(
-    nx, frames, slices, ftab_hbm, itab_hbm, logp, new,
-    fr, sl, ft, it, X, Y, acc, pb, sc, ls, fin, wt, kept, sa, ra, sb, rb,
+    nx, frames, slices, ftab_hbm, logp, new,
+    fr, sl, ft, X, Y, acc, pb, sc, ls, fin, wt, kept, sa, ra, sb, rb,
     fsem, msem, ls_sem, fin_sem, wt_sem, as_, ar, bs, br,
 ):
     K, R, N = fr.shape
@@ -87,21 +86,23 @@
     chunks, half = share // 8, T * 4
     body = half * chunks
 
-    c_ft = pltpu.make_async_copy(ftab_hbm, ft, msem.at[0])
+    quarter = H // 2
+    c_ft = pltpu.make_async_copy(ftab_hbm, ft.at[:, pl.ds(0, quarter)], msem.at[0])
     c_sl = pltpu.make_async_copy(slices, sl, msem.at[1])
-    c_it = pltpu.make_async_copy(itab_hbm, it, msem.at[2])
     for i in range(4):
         for t in range(T):
             part = pl.ds(i * R // 4, R // 4)
             pltpu.make_async_copy(slices.at[t, part], sl.at[t, part], msem.at[1]).start()
-        pltpu.make_async_copy(ftab_hbm.at[i], ft.at[i], msem.at[0]).start()
+        pltpu.make_async_copy(
+            ftab_hbm.at[i], ft.at[i, pl.ds(0, quarter)], msem.at[0]
+        ).start()
 
     def group_copy(g):
         part = pl.ds(g * GROUP, GROUP)
         return pltpu.make_async_copy(frames.at[part], fr.at[part], fsem.at[g])
 
     barrier = pltpu.get_barrier_semaphore()
-    low_z = nz // 2
+    low_z = nz // 4
     lower = z < low_z
     steps = [(i, j) for i in range(low_z) for j in range(nx)]
     steps.sort(key=lambda s: -(min(s[0], low_z - s[0]) + min(s[1], nx - s[1])))
@@ -110,7 +111,7 @@
         return dp, ((z + i) % low_z + upper * low_z) * nx + (x + j) % nx
 
     mine = [at(i, j) for i, j in steps if i or j]
-    opposite = [at(i, j, 1) for i, j in steps]
+    opposite = [at(i, j, u) for u in (2, 3, 1) for i, j in steps]
     family = [((dp + d) % (2 * ny), rot) for d in range(1, 2 * ny)]
     def signal(peer):
         pl.semaphore_signal(barrier, inc=1, device_id=peer, device_id_type=MESH)
@@ -127,10 +128,17 @@
     def _(k):
         pltpu.make_async_copy(frames.at[k], fr.at[k], fsem.at[k // GROUP]).start()
 
-    c_it.start()
-
+
+    c_ft.wait()
+    turn = lax.broadcasted_iota(jnp.int32, (quarter, LANES), 1) % 2
+    turn = (1 - 2 * turn).astype(F32).astype(BF16)
+    for i in range(4):
+        cosine, sine = ft[i, :quarter, :LANES], ft[i, :quarter, LANES:]
+        if i >= 2:
+            cosine, sine = sine, -cosine
+        ft[i, quarter:, :LANES] = cosine * turn
+        ft[i, quarter:, LANES:] = sine * turn
     c_sl.wait()
-    c_ft.wait()
     first = lax.broadcasted_iota(jnp.int32, (R, LANES), 1) == 0
     totals = []
     for t in range(T):
@@ -189,9 +197,8 @@
         [jnp.where(lane == 0, 0.0, cer * scale), cei * jnp.where(lane == 0, edge, scale)], axis=1
     )
     co = jnp.concatenate([cor * scale, coi * scale], axis=1)
-    c_it.wait()
-    u = mm3(ce, it[0], it[1])
-    v = mm3(co, it[2], it[3])
+    u = mm3(ce, ft[0], ft[1], 1)
+    v = mm3(co, ft[2], ft[3], 1)
     anneal = 4.0 / math.sqrt(R * N)
     low, high = anneal * (base + (u + v)), anneal * (base + (u - v))
     sc[:, :H] = low
@@ -209,7 +216,7 @@
 
     def tell(peer):
         pltpu.make_async_remote_copy(
-            ls.at[rot], ls.at[rot], ls_sem.at[0], ls_sem.at[1 + z // low_z],
+            ls.at[rot], ls.at[rot], ls_sem.at[0], ls_sem.at[2 - lower.astype(jnp.int32)],
             device_id=peer, device_id_type=MESH,
         ).start()
 
@@ -217,10 +224,10 @@
         rows = ref.at[pl.ds(0, n)]
         pltpu.make_async_copy(rows, rows, sem).wait()
 
-    def answer():
+    def answer(u):
         return pltpu.make_async_remote_copy(
             fin.at[0], fin.at[0], fin_sem.at[0], fin_sem.at[1],
-            device_id=at(0, 0, 1), device_id_type=MESH,
+            device_id=at(0, 0, u), device_id_type=MESH,
         )
 
     everyone = nz * nx
@@ -231,7 +238,7 @@
 
     @pl.when(jnp.logical_not(lower))
     def _():
-        pl.semaphore_wait(barrier, len(opposite) + len(family))
+        pl.semaphore_wait(barrier, len(steps) + len(family))
         tell(at(0, 0))
 
     for peer in mine:
@@ -243,16 +250,17 @@
     @pl.when(lower)
     def _():
         wait_rows(ls, len(mine), ls_sem.at[1])
-        near_row = lse_of_rows(ls[: everyone // 2])
-        wait_rows(ls, everyone // 2, ls_sem.at[2])
-        far_row = lse_of_rows(ls[everyone // 2 :])
+        near_row = lse_of_rows(ls[: len(steps)])
+        wait_rows(ls, len(opposite), ls_sem.at[2])
+        far_row = lse_of_rows(ls[len(steps) :])
         peak = jnp.maximum(near_row, far_row)
         fin[0] = peak + jnp.log(jnp.exp(near_row - peak) + jnp.exp(far_row - peak))
-        answer().start()
+        for u in (2, 3, 1):
+            answer(u).start()
 
     @pl.when(jnp.logical_not(lower))
     def _():
-        answer().wait_recv()
+        wait_rows(fin, 1, fin_sem.at[1])
 
     lse_row = fin[0]
     lse = jnp.sum(jnp.where(diagonal, lse_row, 0.0), axis=1, keepdims=True)
@@ -382,8 +390,8 @@
         )
     lane = lax.broadcasted_iota(jnp.int32, parts[0].shape, 1)
     ends = jnp.where(lane == 0, edge, scale)
-    u = mm3(jnp.concatenate([parts[0] * ends, parts[1] * ends], axis=1), it[0], it[1])
-    v = mm3(jnp.concatenate([parts[2] * scale, parts[3] * scale], axis=1), it[2], it[3])
+    u = mm3(jnp.concatenate([parts[0] * ends, parts[1] * ends], axis=1), ft[0], ft[1], 1)
+    v = mm3(jnp.concatenate([parts[2] * scale, parts[3] * scale], axis=1), ft[2], ft[3], 1)
     owned = pl.ds(pl.multiple_of(dp * share, 8), share)
     for t in range(T):
         rows = slice(t * share, (t + 1) * share)
@@ -395,7 +403,7 @@
 
     @pl.when(lower)
     def _():
-        answer().wait_send()
+        wait_rows(ls, 3, fin_sem.at[0])
 
     @pl.when(jnp.logical_not(lower))
     def _():
@@ -427,7 +435,7 @@
     assert ny == 4 and R // (2 * ny) == 16
     share = R // (2 * ny)
     body = T * 4 * (share // 8)
-    forward, inverse = packed_tables(N)
+    forward = packed_tables(N)
     hbm = pl.BlockSpec(memory_space=pltpu.HBM)
     vmem = pl.BlockSpec(memory_space=pltpu.VMEM)
     dma = pltpu.SemaphoreType.DMA
@@ -437,12 +445,11 @@
             jax.ShapeDtypeStruct((K * T * N // LANES, LANES), F32),
             jax.ShapeDtypeStruct((T, share, N), F32),
         ),
-        in_specs=[hbm] * 4,
+        in_specs=[hbm] * 3,
         out_specs=(vmem, vmem),
         scratch_shapes=[
             pltpu.VMEM((K, R, N), jnp.int32),
             pltpu.VMEM((T, R, N), F32),
-            pltpu.VMEM((4, N // 2, N // 2), BF16),
             pltpu.VMEM((4, N // 2, N // 2), BF16),
             pltpu.VMEM((K, 6, R, LANES), F32),
             pltpu.VMEM((T, 6, R, LANES), F32),
@@ -458,7 +465,7 @@
             pltpu.VMEM((6, body // 2, 8, LANES), F32),
             pltpu.VMEM((6, body // 2, 8, LANES), F32),
             dma((K // GROUP,)),
-            dma((3,)),
+            dma((2,)),
             dma((3,)),
             dma((2,)),
             dma((2,)),
@@ -470,7 +477,7 @@
         compiler_params=pltpu.CompilerParams(
             collective_id=0, has_side_effects=True, vmem_limit_bytes=32 << 20
         ),
-    )(*(pltpu.with_memory_space_constraint(v, pltpu.HBM) for v in (frames, slices, jnp.asarray(forward), jnp.asarray(inverse))))
+    )(*(pltpu.with_memory_space_constraint(v, pltpu.HBM) for v in (frames, slices, jnp.asarray(forward))))
     logp, new = pl.pallas_call(
         hand_over,
         out_shape=(

time: 33.7 us -> 33.6 us (level)
  no operation moved by 1% of the time
where the time goes in v4:
time: 33.6 us; the launch traced here: 33.5 us
  Pallas kernels  32.8 us (98%)
  between operations  0.64 us (2%)
    pallas_call x1, Pallas kernels, on_device(): pl.pallas_call(functools.partial(kernel, nx), out_shape=(jax.ShapeDtypeSt...  32.1 us

profile of v4, /device:TPU:1, one launch (start us, length us, event | category | flops | bytes accessed | tf_op | source)
XLA Modules:
  0.0 33.5 jit_solution(834928203307312993)
XLA Ops:
  0.6 32.1 %shard_map.50 = (f32[128,128]{1,0:T(8,128)S(1)}, f32[2,16,512]{2,1,0:T(8,128)S(1)}) custom-call(s32[16,128,512]{2,1,0:T(8,128)} %frames.1, f32[2,128,512]{2,1,0:T(8,128)} %slices.1, bf16[4,128,256]{2,1,0:T(8,128)(2,1)} %constant.2.clone.ftab_hbm), custom_call_target="tpu_custom_call" | custom-call | tf_op jit(solution)/shard_map/pallas_call | solution.py:442
  32.8 0.7 %shard_map.51 = (f32[128,128]{1,0:T(8,128)}, f32[2,16,512]{2,1,0:T(8,128)}) custom-call(f32[128,128]{1,0:T(8,128)S(1)} %get-tuple-element.6.logp, f32[2,16,512]{2,1,0:T(8,128)S(1)} %get-tuple-element.7.new), custom_call_target="tpu_custom_call" | custom-call | tf_op jit(solution)/shard_map/pallas_call | solution.py:481
